TPU v7x, 32 devices: a whole 2x2x4 slice. The times are simulated.
32 devices in a mesh: lat: 4 (over y, x), lon: 2 (over core), lev: 4 (over z).
Axes of the slice: x: 2, y: 2, z: 4, core: 2. Of those that a mesh axis runs over, the one named last changes fastest.
Arguments:
- winds: float32 [16, 72, 2, 256], P('lat', 'lev', None, 'lon'), may hold values from -0.45 to 0.45
- mixing: float32 [16, 72, 72], P(('lat', 'lev')), may hold values from -0.12 to 0.7, as said below
- kernels: float32 [2048, 72], P(('lat', 'lon', 'lev')), may hold values from 0.2 to 1.2
- residuals: float32 [2048, 16], P(('lat', 'lon', 'lev')), may hold values from -6 to 6
- columns: int32 [2048], P(('lat', 'lon', 'lev')), may hold values from 0 to 127
- owners: int32 [2048, 1], P(('lat', 'lon', 'lev')), may hold values from 0 to 7; in each aligned block of 64 rows (0 to 63, 64 to 127, ...) at most 16 rows name the same one
- live_counts: int32 [32], P(('lat', 'lon', 'lev')), may hold values from 32 to 64, as said below
Outputs:
- gradient: float32 [16, 72, 16, 256], P('lat', 'lev', None, 'lon')
Inputs may be any that keep to these rules, and one draw needn't show every extreme that they name: Diagonal entries of every mixing matrix lie between 0.38 and 0.7, off-diagonal entries between -0.12 and 0.12, in every draw. The first live_counts[b] slots of device b's retrievals are live; some device has all 64 live. Column index row by row over the owner's 1 row of 128 columns. `owners`: at most 16 slots of one device name the same owner.
All inputs are finite; a program needn't handle non-finite values.
Results may differ from a plain program's by a relative error of at most 0.00022.
Values sent between devices are 32-bit elements; how exact they have to be, the bound alone decides.
A program may use at most 64 MiB of HBM per device.

v0:
```python
import jax
import jax.numpy as jnp
from jax import lax
from jax.sharding import PartitionSpec as P

STEPS = 4


def with_halo(block, sides, width):
    for axis, dim in sides:
        count = lax.axis_size(axis)
        forward = [(i, i + 1) for i in range(count - 1)]
        forward.append((count - 1, 0))
        backward = [(target, source) for source, target in forward]
        low = lax.ppermute(
            lax.slice_in_dim(block, block.shape[dim] - width, None, axis=dim), axis, forward
        )
        high = lax.ppermute(lax.slice_in_dim(block, 0, width, axis=dim), axis, backward)
        block = jnp.concatenate([low, block, high], axis=dim)
    return block


def transport(padded, winds, at_first, at_last):
    centre = padded[1:-1, :, :, 1:-1]
    east_side = padded[1:-1, :, :, 2:]
    west_side = padded[1:-1, :, :, :-2]
    north_side = padded[2:, :, :, 1:-1]
    south_side = padded[:-2, :, :, 1:-1]
    north_side = jnp.concatenate([north_side[:-1], jnp.where(at_last, centre, north_side)], axis=0)
    south_side = jnp.concatenate([jnp.where(at_first, centre, south_side), south_side[1:]], axis=0)
    zonal_wind = winds[:, :, 0:1, :]
    merid_wind = winds[:, :, 1:2, :]
    return (
        centre
        + jnp.maximum(zonal_wind, 0.0) * (east_side - centre)
        + jnp.minimum(zonal_wind, 0.0) * (centre - west_side)
        + jnp.maximum(merid_wind, 0.0) * (north_side - centre)
        + jnp.minimum(merid_wind, 0.0) * (centre - south_side)
    )


def mix_back(mixing, adjoint):
    return jnp.einsum("rjk,rjtl->rktl", mixing, adjoint, precision=lax.Precision.HIGHEST)


def deposit(summed, kern_rows, resid_part, col_ids):
    contrib = (kern_rows[:, :, None] * resid_part[:, None, :]).reshape(kern_rows.shape[0], -1)
    return summed.at[col_ids].add(contrib)


def shards(winds, mixing, kernels, residuals, columns, owners, live_counts):
    levels = mixing.shape[1]
    tracers = residuals.shape[1]
    slab_rows = mixing.shape[0]
    tile_cols = winds.shape[3]
    row_count = kernels.shape[0]
    lat_size = lax.axis_size("lat")
    lev_size = lax.axis_size("lev")
    my_index = lax.axis_index("lon") * lev_size + lax.axis_index("lev")
    live_mask = (jnp.arange(row_count) < live_counts[0]).astype(jnp.float32)
    resid_rows = residuals * live_mask[:, None]
    owner_ids = owners[:, 0]
    running = jnp.zeros((slab_rows * tile_cols, levels * tracers), jnp.float32)
    kern_part = lax.all_gather(kernels, ("lon", "lev"), axis=0, tiled=True)
    resid_part = lax.all_gather(resid_rows, ("lon", "lev"), axis=0, tiled=True)
    col_part = lax.all_gather(columns, ("lon", "lev"), axis=0, tiled=True)
    owner_part = lax.all_gather(owner_ids, ("lon", "lev"), axis=0, tiled=True)
    keep_mask = (owner_part == my_index).astype(jnp.float32)
    running = deposit(running, kern_part, resid_part * keep_mask[:, None], col_part)
    adjoint = running.reshape(slab_rows, tile_cols, levels, tracers).transpose(0, 2, 3, 1)
    wind_cols = lax.all_to_all(winds, "lev", split_axis=0, concat_axis=1, tiled=True)
    lat_pos = lax.axis_index("lat")
    lev_pos = lax.axis_index("lev")
    at_first = (lat_pos == 0) & (lev_pos == 0)
    at_last = (lat_pos == lat_size - 1) & (lev_pos == lev_size - 1)
    for sweep_index in range(STEPS):
        mixed = mix_back(mixing, adjoint)
        padded = with_halo(mixed, ((("lat", "lev"), 0), ("lon", 3)), 1)
        adjoint = transport(padded, wind_cols, at_first, at_last)
    gradient = lax.all_to_all(adjoint, "lev", split_axis=1, concat_axis=0, tiled=True)
    return gradient


def solution(mesh):
    return jax.shard_map(
        shards,
        mesh=mesh,
        in_specs=(
            P("lat", "lev", None, "lon"),
            P(("lat", "lev"), None, None),
            P(("lat", "lon", "lev"), None),
            P(("lat", "lon", "lev"), None),
            P(("lat", "lon", "lev")),
            P(("lat", "lon", "lev"), None),
            P(("lat", "lon", "lev")),
        ),
        out_specs=P("lat", "lev", None, "lon"),
        check_vma=False,
    )
```

profile of v0, /device:TPU:0, one launch (start us, length us, event | category | flops | bytes accessed | tf_op | source)
XLA Modules:
  0.0 261.8 jit_solution(14220002208314231462)
XLA Ops:
  4.2 10.7 %all-reduce.2 = (s32[512]{0:T(512)S(1)}, s32[512]{0:T(512)S(1)}) all-reduce(s32[512]{0:T(512)S(1)} %dynamic-update-slice, s32[512]{0:T(512)S(1)} %bitcast_dynamic-update-slice_fusion), channel_id=1, replica_groups=mesh['lat'=4,'lon'=2,'lev'=4] {'lon','lev'}, use_global_device_ids=true, to_apply=%add | all-reduce | flops 1024 | bytes 8192
  15.6 23.9 %all-gather.1 = f32[8,64,16]{1,2,0:T(8,128)S(1)} all-gather(f32[1,64,16]{1,2,0:T(8,128)S(1)} %multiply_bitcast_fusion), channel_id=1, replica_groups=mesh['lat'=4,'lon'=2,'lev'=4] {'lon','lev'}, dimensions={0}, use_global_device_ids=true | all-gather | bytes 36864 | tf_op jit(solution)/shard_map/all_gather | solution.py:65
  39.6 25.4 %all_gather.13 = f32[512,72]{1,0:T(8,128)S(1)} all-gather(f32[64,72]{1,0:T(8,128)} %param.9), channel_id=1, replica_groups=mesh['lat'=4,'lon'=2,'lev'=4] {'lon','lev'}, dimensions={0}, use_global_device_ids=true | all-gather | bytes 165888 | tf_op jit(solution)/shard_map/all_gather | solution.py:64
  65.5 2.0 copy.39
  67.5 6.4 %scatter_custom_fusion = f32[128,1152]{1,0:T(8,128)S(1)} fusion(s32[512]{0:T(512)S(1)} %compare_select_fusion, f32[512,1152]{1,0:T(8,128)} %copy.39, f32[]{:T(128)} %constant.8.clone.1), kind=kCustom, calls=%fused_computation.104 | custom fusion | flops 589824 | bytes 590336 | tf_op jit(solution)/shard_map/scatter-add | solution.py:48
  75.1 3.5 %collective-permute-start.1 = (f32[1,72,16,128]{3,1,2,0:T(8,128)S(1)}, f32[1,72,16,128]{3,1,2,0:T(8,128)S(1)}, u32[]{:S(2)}, u32[]{:S(2)}) collective-permute-start(f32[1,72,16,128]{3,1,2,0:T(8,128)S(1)} %convolution_bitcast_fusion.3), channel_id=1, source_target_pairs={{1,0},{2,1},{3,2},{8,3},{9,8},{10,9},{11,10},{16,11},{17,16},{18,1... | collective-permute-start | bytes 1769480 | tf_op jit(solution)/shard_map/ppermute | solution.py:18
  78.6 4.1 %all-to-all-start = ((f32[4,18,2,128]{3,2,1,0:T(2,128)}), f32[4,18,2,128]{3,2,1,0:T(2,128)S(1)}, u32[]{:S(2)}, u32[]{:S(2)}) async-start(f32[4,18,2,128]{3,2,1,0:T(2,128)} %param.7), calls=%async_computation | async-start | bytes 147456 | tf_op jit(solution)/shard_map/all_to_all | solution.py:71
  82.7 22.6 %all-to-all-done = f32[4,18,2,128]{3,2,1,0:T(2,128)S(1)} async-done(((f32[4,18,2,128]{3,2,1,0:T(2,128)}), f32[4,18,2,128]{3,2,1,0:T(2,128)S(1)}, u32[]{:S(2)}, u32[]{:S(2)}) %all-to-all-start) | async-done | bytes 73760 | tf_op jit(solution)/shard_map/all_to_all | solution.py:71
  109.0 2.0 copy.44
  115.5 2.7 %convolution_bitcast_fusion.2 = f32[1,72,16,128]{3,1,2,0:T(8,128)S(1)} fusion(f32[1,72,16,128]{3,1,2,0:T(8,128)S(1)} %convolution_bitcast_fusion.3, f32[1,72,16,128]{3,1,2,0:T(8,128)} %copy-done.1, f32[1,72,16,128]{3,1,2,0:T(8,128)} %copy-done.2, f32[3,72,16,1]{3,1,2,0:T(8,128)} %copy.47, f32[3,72,16,1]{3,1,2,0:T(8,128)S(1)} %copy.45, ...), kind=kOutput, calls=%fused_computation.7 | convolution fusion | flops 130351104 | bytes 2555138 | tf_op jit(solution)/shard_map/rjk,rjtl->rktl/dot_general | solution.py:43
  118.2 4.1 %collective-permute-start.5 = (f32[1,72,16,128]{3,1,2,0:T(8,128)S(1)}, f32[1,72,16,128]{3,1,2,0:T(8,128)S(1)}, u32[]{:S(2)}, u32[]{:S(2)}) collective-permute-start(f32[1,72,16,128]{3,1,2,0:T(8,128)S(1)} %convolution_bitcast_fusion.2), channel_id=1, source_target_pairs={{1,0},{2,1},{3,2},{8,3},{9,8},{10,9},{11,10},{16,11},{17,16},{18,1... | collective-permute-start | bytes 1769480 | tf_op jit(solution)/shard_map/ppermute | solution.py:18
  122.3 13.7 %collective-permute-done.5 = f32[1,72,16,128]{3,1,2,0:T(8,128)S(1)} collective-permute-done((f32[1,72,16,128]{3,1,2,0:T(8,128)S(1)}, f32[1,72,16,128]{3,1,2,0:T(8,128)S(1)}, u32[]{:S(2)}, u32[]{:S(2)}) %collective-permute-start.5) | collective-permute-done | bytes 589856 | tf_op jit(solution)/shard_map/ppermute | solution.py:18
  136.0 13.2 %collective-permute-done.4 = f32[1,72,16,128]{3,1,2,0:T(8,128)S(1)} collective-permute-done((f32[1,72,16,128]{3,1,2,0:T(8,128)S(1)}, f32[1,72,16,128]{3,1,2,0:T(8,128)S(1)}, u32[]{:S(2)}, u32[]{:S(2)}) %collective-permute-start.4) | collective-permute-done | bytes 589856 | tf_op jit(solution)/shard_map/ppermute | solution.py:15
  152.0 2.0 copy.50
  157.9 2.7 %convolution_bitcast_fusion.1 = f32[1,72,16,128]{3,1,2,0:T(8,128)S(1)} fusion(f32[1,72,16,128]{3,1,2,0:T(8,128)S(1)} %convolution_bitcast_fusion.2, f32[1,72,16,128]{3,1,2,0:T(8,128)} %copy-done.4, f32[1,72,16,128]{3,1,2,0:T(8,128)} %copy-done.6, f32[3,72,16,1]{3,1,2,0:T(8,128)} %copy.53, f32[3,72,16,1]{3,1,2,0:T(8,128)S(1)} %copy.51, ...), kind=kOutput, calls=%fused_computation.6 | convolution fusion | flops 130351104 | bytes 2555138 | tf_op jit(solution)/shard_map/rjk,rjtl->rktl/dot_general | solution.py:43
  162.7 13.8 %collective-permute-done.9 = f32[1,72,16,128]{3,1,2,0:T(8,128)S(1)} collective-permute-done((f32[1,72,16,128]{3,1,2,0:T(8,128)S(1)}, f32[1,72,16,128]{3,1,2,0:T(8,128)S(1)}, u32[]{:S(2)}, u32[]{:S(2)}) %collective-permute-start.9) | collective-permute-done | bytes 589856 | tf_op jit(solution)/shard_map/ppermute | solution.py:18
  176.5 12.8 %collective-permute-done.8 = f32[1,72,16,128]{3,1,2,0:T(8,128)S(1)} collective-permute-done((f32[1,72,16,128]{3,1,2,0:T(8,128)S(1)}, f32[1,72,16,128]{3,1,2,0:T(8,128)S(1)}, u32[]{:S(2)}, u32[]{:S(2)}) %collective-permute-start.8) | collective-permute-done | bytes 589856 | tf_op jit(solution)/shard_map/ppermute | solution.py:15
  192.1 2.0 copy.55
  197.9 2.7 %convolution_bitcast_fusion = f32[1,72,16,128]{3,1,2,0:T(8,128)S(1)} fusion(f32[1,72,16,128]{3,1,2,0:T(8,128)S(1)} %convolution_bitcast_fusion.1, f32[1,72,16,128]{3,1,2,0:T(8,128)} %copy-done.5, f32[1,72,16,128]{3,1,2,0:T(8,128)} %copy-done.7, f32[3,72,16,1]{3,1,2,0:T(8,128)} %copy.58, f32[3,72,16,1]{3,1,2,0:T(8,128)S(1)} %copy.56, ...), kind=kOutput, calls=%fused_computation.5 | convolution fusion | flops 130351104 | bytes 2555138 | tf_op jit(solution)/shard_map/rjk,rjtl->rktl/dot_general | solution.py:43
  200.6 2.7 %collective-permute-start.13 = (f32[1,72,16,128]{3,1,2,0:T(8,128)S(1)}, f32[1,72,16,128]{3,1,2,0:T(8,128)S(1)}, u32[]{:S(2)}, u32[]{:S(2)}) collective-permute-start(f32[1,72,16,128]{3,1,2,0:T(8,128)S(1)} %convolution_bitcast_fusion), channel_id=1, source_target_pairs={{1,0},{2,1},{3,2},{8,3},{9,8},{10,9},{11,10},{16,11},{17,16},{18,1... | collective-permute-start | bytes 1769480 | tf_op jit(solution)/shard_map/ppermute | solution.py:18
  203.4 13.7 %collective-permute-done.13 = f32[1,72,16,128]{3,1,2,0:T(8,128)S(1)} collective-permute-done((f32[1,72,16,128]{3,1,2,0:T(8,128)S(1)}, f32[1,72,16,128]{3,1,2,0:T(8,128)S(1)}, u32[]{:S(2)}, u32[]{:S(2)}) %collective-permute-start.13) | collective-permute-done | bytes 589856 | tf_op jit(solution)/shard_map/ppermute | solution.py:18
  217.1 14.2 %collective-permute-done.12 = f32[1,72,16,128]{3,1,2,0:T(8,128)S(1)} collective-permute-done((f32[1,72,16,128]{3,1,2,0:T(8,128)S(1)}, f32[1,72,16,128]{3,1,2,0:T(8,128)S(1)}, u32[]{:S(2)}, u32[]{:S(2)}) %collective-permute-start.12) | collective-permute-done | bytes 589856 | tf_op jit(solution)/shard_map/ppermute | solution.py:15
  234.1 2.0 copy.60
  241.9 19.1 %all_to_all.24 = f32[1,72,16,128]{3,2,0,1:T(8,128)S(1)} all-to-all(f32[1,72,16,128]{3,2,0,1:T(8,128)S(1)} %copy.64), channel_id=1, replica_groups=mesh['lat'=4,'lon'=2,'lev'=4] {'lev'}, dimensions={1} | all-to-all | bytes 1179648 | tf_op jit(solution)/shard_map/all_to_all | solution.py:80
  (80 shorter events, 38.0 us)
Async XLA Ops:
  0.0 74.2 %copy-start = (f32[1,72,72]{2,1,0:T(8,128)S(1)}, f32[1,72,72]{2,1,0:T(8,128)}, u32[]{:S(2)}) copy-start(f32[1,72,72]{2,1,0:T(8,128)} %param.8) | copy-start | bytes 62212
  75.1 30.3 %collective-permute-start.1 = (f32[1,72,16,128]{3,1,2,0:T(8,128)S(1)}, f32[1,72,16,128]{3,1,2,0:T(8,128)S(1)}, u32[]{:S(2)}, u32[]{:S(2)}) collective-permute-start(f32[1,72,16,128]{3,1,2,0:T(8,128)S(1)} %convolution_bitcast_fusion.3), channel_id=1, source_target_pairs={{1,0},{2,1},{3,2},{8,3},{9,8},{10,9},{11,10},{16,11},{17,16},{18,1... | collective-permute-start | bytes 1769480 | tf_op jit(solution)/shard_map/ppermute | solution.py:18
  78.6 27.1 %collective-permute-start = (f32[1,72,16,128]{3,1,2,0:T(8,128)S(1)}, f32[1,72,16,128]{3,1,2,0:T(8,128)S(1)}, u32[]{:S(2)}, u32[]{:S(2)}) collective-permute-start(f32[1,72,16,128]{3,1,2,0:T(8,128)S(1)} %convolution_bitcast_fusion.3), channel_id=1, source_target_pairs={{0,1},{1,2},{2,3},{3,8},{8,9},{9,10},{10,11},{11,16},{16,17},{17,1... | collective-permute-start | bytes 1769480 | tf_op jit(solution)/shard_map/ppermute | solution.py:15
  78.6 26.7 %all-to-all-start = ((f32[4,18,2,128]{3,2,1,0:T(2,128)}), f32[4,18,2,128]{3,2,1,0:T(2,128)S(1)}, u32[]{:S(2)}, u32[]{:S(2)}) async-start(f32[4,18,2,128]{3,2,1,0:T(2,128)} %param.7), calls=%async_computation | async-start | bytes 147456 | tf_op jit(solution)/shard_map/all_to_all | solution.py:71
  105.4 0.8 copy-start.1
  106.3 0.8 copy-start.2
  111.6 2.0 collective-permute-start.3
  111.7 1.3 collective-permute-start.2
  118.2 17.8 %collective-permute-start.5 = (f32[1,72,16,128]{3,1,2,0:T(8,128)S(1)}, f32[1,72,16,128]{3,1,2,0:T(8,128)S(1)}, u32[]{:S(2)}, u32[]{:S(2)}) collective-permute-start(f32[1,72,16,128]{3,1,2,0:T(8,128)S(1)} %convolution_bitcast_fusion.2), channel_id=1, source_target_pairs={{1,0},{2,1},{3,2},{8,3},{9,8},{10,9},{11,10},{16,11},{17,16},{18,1... | collective-permute-start | bytes 1769480 | tf_op jit(solution)/shard_map/ppermute | solution.py:18
  122.3 27.0 %collective-permute-start.4 = (f32[1,72,16,128]{3,1,2,0:T(8,128)S(1)}, f32[1,72,16,128]{3,1,2,0:T(8,128)S(1)}, u32[]{:S(2)}, u32[]{:S(2)}) collective-permute-start(f32[1,72,16,128]{3,1,2,0:T(8,128)S(1)} %convolution_bitcast_fusion.2), channel_id=1, source_target_pairs={{0,1},{1,2},{2,3},{3,8},{8,9},{9,10},{10,11},{11,16},{16,17},{17,1... | collective-permute-start | bytes 1769480 | tf_op jit(solution)/shard_map/ppermute | solution.py:15
  136.0 13.2 %copy-start.4 = (f32[1,72,16,128]{3,1,2,0:T(8,128)}, f32[1,72,16,128]{3,1,2,0:T(8,128)S(1)}, u32[]{:S(2)}) copy-start(f32[1,72,16,128]{3,1,2,0:T(8,128)S(1)} %collective-permute-done.5) | copy-start | bytes 1769476
  149.2 0.8 copy-start.6
  154.1 1.2 collective-permute-start.6
  154.7 1.4 collective-permute-start.7
  160.6 15.9 %collective-permute-start.9 = (f32[1,72,16,128]{3,1,2,0:T(8,128)S(1)}, f32[1,72,16,128]{3,1,2,0:T(8,128)S(1)}, u32[]{:S(2)}, u32[]{:S(2)}) collective-permute-start(f32[1,72,16,128]{3,1,2,0:T(8,128)S(1)} %convolution_bitcast_fusion.1), channel_id=1, source_target_pairs={{1,0},{2,1},{3,2},{8,3},{9,8},{10,9},{11,10},{16,11},{17,16},{18,1... | collective-permute-start | bytes 1769480 | tf_op jit(solution)/shard_map/ppermute | solution.py:18
  162.4 26.9 %collective-permute-start.8 = (f32[1,72,16,128]{3,1,2,0:T(8,128)S(1)}, f32[1,72,16,128]{3,1,2,0:T(8,128)S(1)}, u32[]{:S(2)}, u32[]{:S(2)}) collective-permute-start(f32[1,72,16,128]{3,1,2,0:T(8,128)S(1)} %convolution_bitcast_fusion.1), channel_id=1, source_target_pairs={{0,1},{1,2},{2,3},{3,8},{8,9},{9,10},{10,11},{11,16},{16,17},{17,1... | collective-permute-start | bytes 1769480 | tf_op jit(solution)/shard_map/ppermute | solution.py:15
  176.5 12.8 %copy-start.5 = (f32[1,72,16,128]{3,1,2,0:T(8,128)}, f32[1,72,16,128]{3,1,2,0:T(8,128)S(1)}, u32[]{:S(2)}) copy-start(f32[1,72,16,128]{3,1,2,0:T(8,128)S(1)} %collective-permute-done.9) | copy-start | bytes 1769476
  189.3 0.8 copy-start.7
  194.1 1.2 collective-permute-start.10
  194.7 1.4 collective-permute-start.11
  200.6 16.4 %collective-permute-start.13 = (f32[1,72,16,128]{3,1,2,0:T(8,128)S(1)}, f32[1,72,16,128]{3,1,2,0:T(8,128)S(1)}, u32[]{:S(2)}, u32[]{:S(2)}) collective-permute-start(f32[1,72,16,128]{3,1,2,0:T(8,128)S(1)} %convolution_bitcast_fusion), channel_id=1, source_target_pairs={{1,0},{2,1},{3,2},{8,3},{9,8},{10,9},{11,10},{16,11},{17,16},{18,1... | collective-permute-start | bytes 1769480 | tf_op jit(solution)/shard_map/ppermute | solution.py:18
  203.3 27.9 %collective-permute-start.12 = (f32[1,72,16,128]{3,1,2,0:T(8,128)S(1)}, f32[1,72,16,128]{3,1,2,0:T(8,128)S(1)}, u32[]{:S(2)}, u32[]{:S(2)}) collective-permute-start(f32[1,72,16,128]{3,1,2,0:T(8,128)S(1)} %convolution_bitcast_fusion), channel_id=1, source_target_pairs={{0,1},{1,2},{2,3},{3,8},{8,9},{9,10},{10,11},{11,16},{16,17},{17,1... | collective-permute-start | bytes 1769480 | tf_op jit(solution)/shard_map/ppermute | solution.py:15
  236.1 1.2 collective-permute-start.14
  236.8 1.4 collective-permute-start.15
  (1 other events, 0.8 us)
where the time goes:
time: 262 us
  waiting for transfers between devices  106 us (40%)
  blocking collectives  79.2 us (30%)
  local copies, waits for them, and re-layouts  37.5 us (14%)
  starting transfers between devices  18.9 us (7%)
  other arithmetic  9.9 us (4%)
  matrix products  8.81 us (3%)
    ppermute x8, waiting for transfers between devices, with_halo(): lax.ppermute(lax.slice_in_dim(block, 0, width, axis=dim), axis, backward)  42.3 us
    ppermute x8, waiting for transfers between devices, with_halo(): lax.ppermute(lax.slice_in_dim(block, block.shape[dim] - width, None, axis...  41 us
    all_gather x1, blocking collectives, shards(): kern_part = lax.all_gather(kernels, ('lon', 'lev'), axis=0, tiled=True)  25.4 us
    all_gather x1, blocking collectives, shards(): resid_part = lax.all_gather(resid_rows, ('lon', 'lev'), axis=0, tiled=True)  23.9 us
    all_to_all x1, waiting for transfers between devices, shards(): lax.all_to_all(winds, 'lev', split_axis=0, concat_axis=1, tiled=True)  22.6 us
    all_to_all x1, blocking collectives, shards(): lax.all_to_all(adjoint, 'lev', split_axis=1, concat_axis=0, tiled=True)  19.1 us
    slice x8, local copies, waits for them, and re-layouts, with_halo(): lax.slice_in_dim(block, 0, width, axis=dim)  15.4 us
    ppermute x8, starting transfers between devices, with_halo(): lax.ppermute(lax.slice_in_dim(block, 0, width, axis=dim), axis, backward)  12.8 us
  transfers between devices with their start and end apart: 17, of which 15 were waited for; matrix products, arithmetic and copies ran while one was open for 2% of the time, Pallas kernels for 0%

commit v1 on v0

--- a/solution.py
+++ b/solution.py
@@ -62,7 +62,29 @@
     owner_ids = owners[:, 0]
     running = jnp.zeros((slab_rows * tile_cols, levels * tracers), jnp.float32)
     kern_part = lax.all_gather(kernels, ("lon", "lev"), axis=0, tiled=True)
-    resid_part = lax.all_gather(resid_rows, ("lon", "lev"), axis=0, tiled=True)
+    length, here, rows = (
+        lax.axis_size(("lon", "lev")),
+        lax.axis_index(("lon", "lev")),
+        resid_rows.shape[0],
+    )
+    forward_2 = [(i_2, (i_2 + 1) % length) for i_2 in range(length)]
+    behind = [(i_2, (i_2 - 1) % length) for i_2 in range(length)]
+    resid_part = jnp.zeros(
+        (*resid_rows.shape[:0], length * rows, *resid_rows.shape[0 + 1 :]), resid_rows.dtype
+    )
+    resid_part = lax.dynamic_update_slice_in_dim(resid_part, resid_rows, here * rows, axis=0)
+    from_left = from_right = resid_rows
+    half = length // 2
+    for step in range(1, half + 1):
+        from_left = lax.ppermute(from_left, ("lon", "lev"), forward_2)
+        resid_part = lax.dynamic_update_slice_in_dim(
+            resid_part, from_left, (here - step) % length * rows, axis=0
+        )
+        if step < length - half:
+            from_right = lax.ppermute(from_right, ("lon", "lev"), behind)
+            resid_part = lax.dynamic_update_slice_in_dim(
+                resid_part, from_right, (here + step) % length * rows, axis=0
+            )
     col_part = lax.all_gather(columns, ("lon", "lev"), axis=0, tiled=True)
     owner_part = lax.all_gather(owner_ids, ("lon", "lev"), axis=0, tiled=True)
     keep_mask = (owner_part == my_index).astype(jnp.float32)

time: 262 us -> 255 us (0.973)
  blocking collectives: 79.2 us -> 53.9 us
  starting transfers between devices: 18.9 us -> 30.1 us
  waiting for transfers between devices: 106 us -> 110 us
    all_gather x1 -> x0, blocking collectives: 23.9 us -> none  [shards(): resid_part = lax.all_gather(resid_rows, ('lon', 'lev'), axis=0, tiled=True)]
    ppermute x0 -> x7, starting transfers between devices: none -> 11.3 us  [the longest x3 8.68 us: shards(): from_right = lax.ppermute(from_right, ('lon', 'lev'), behind)]
    ppermute x0 -> x7, waiting for transfers between devices: none -> 4.25 us  [the longest x4 2.62 us: shards(): from_left = lax.ppermute(from_left, ('lon', 'lev'), forward_2)]
    unnamed x23 -> x22, local copies, waits for them, and re-layouts: 7.56 us -> 7.78 us
  transfers between devices with their start and end apart: 17 -> 24, of which waited for: 15 -> 16; matrix products, arithmetic and copies ran while one was open for 2% -> 4% of each run, Pallas kernels for 0% -> 0%
where the time goes in v1:
time: 255 us; the launch traced here: 254 us
  waiting for transfers between devices  110 us (43%)
  blocking collectives  53.9 us (21%)
  local copies, waits for them, and re-layouts  39.8 us (16%)
  starting transfers between devices  30.1 us (12%)
  other arithmetic  9.9 us (4%)
  matrix products  8.81 us (3%)
    ppermute x8, waiting for transfers between devices, with_halo(): lax.ppermute(lax.slice_in_dim(block, 0, width, axis=dim), axis, backward)  42.5 us
    ppermute x8, waiting for transfers between devices, with_halo(): lax.ppermute(lax.slice_in_dim(block, block.shape[dim] - width, None, axis...  40.4 us
    all_gather x1, blocking collectives, shards(): kern_part = lax.all_gather(kernels, ('lon', 'lev'), axis=0, tiled=True)  25.5 us
    all_to_all x1, waiting for transfers between devices, shards(): lax.all_to_all(winds, 'lev', split_axis=0, concat_axis=1, tiled=True)  22.7 us
    all_to_all x1, blocking collectives, shards(): lax.all_to_all(adjoint, 'lev', split_axis=1, concat_axis=0, tiled=True)  19.1 us
    slice x8, local copies, waits for them, and re-layouts, with_halo(): lax.slice_in_dim(block, 0, width, axis=dim)  15.3 us
    ppermute x8, starting transfers between devices, with_halo(): lax.ppermute(lax.slice_in_dim(block, 0, width, axis=dim), axis, backward)  12.7 us
    unnamed x1, blocking collectives  9.34 us
  transfers between devices with their start and end apart: 24, of which 16 were waited for; matrix products, arithmetic and copies ran while one was open for 4% of the time, Pallas kernels for 0%

profile of v1, /device:TPU:0, one launch (start us, length us, event | category | flops | bytes accessed | tf_op | source)
XLA Modules:
  0.0 254.0 jit_solution(2032868492971986656)
XLA Ops:
  1.4 4.5 %collective-permute-start.1 = (f32[64,16]{0,1:T(8,128)S(1)}, f32[64,16]{0,1:T(8,128)S(1)}, u32[]{:S(2)}, u32[]{:S(2)}) collective-permute-start(f32[64,16]{0,1:T(8,128)S(1)} %broadcast_multiply_fusion.2), channel_id=1, source_target_pairs={{0,7},{1,0},{2,1},{3,2},{4,3},{5,4},{6,5},{7,6},{8,15},{9,8},{10,9... | collective-permute-start | bytes 12296 | tf_op jit(solution)/shard_map/ppermute | solution.py:84
  9.4 9.3 %all-reduce.2 = (s32[512]{0:T(512)S(1)}, s32[512]{0:T(512)S(1)}) all-reduce(s32[512]{0:T(512)S(1)} %dynamic-update-slice, s32[512]{0:T(512)S(1)} %bitcast_dynamic-update-slice_fusion), channel_id=1, replica_groups=mesh['lat'=4,'lon'=2,'lev'=4] {'lon','lev'}, use_global_device_ids=true, to_apply=%add | all-reduce | flops 1024 | bytes 8192
  18.7 2.1 collective-permute-start.2
  20.8 25.5 %all_gather.10 = f32[512,72]{1,0:T(8,128)S(1)} all-gather(f32[64,72]{1,0:T(8,128)} %param.9), channel_id=1, replica_groups=mesh['lat'=4,'lon'=2,'lev'=4] {'lon','lev'}, dimensions={0}, use_global_device_ids=true | all-gather | bytes 165888 | tf_op jit(solution)/shard_map/all_gather | solution.py:64
  49.9 2.7 %collective-permute-start.5 = (f32[64,16]{0,1:T(8,128)S(1)}, f32[64,16]{0,1:T(8,128)S(1)}, u32[]{:S(2)}, u32[]{:S(2)}) collective-permute-start(f32[64,16]{0,1:T(8,128)S(1)} %collective-permute-done.3), channel_id=1, source_target_pairs={{0,7},{1,0},{2,1},{3,2},{4,3},{5,4},{6,5},{7,6},{8,15},{9,8},{10,9... | collective-permute-start | bytes 12296 | tf_op jit(solution)/shard_map/ppermute | solution.py:84
  54.9 2.6 %collective-permute-done.6 = f32[64,16]{0,1:T(8,128)S(1)} collective-permute-done((f32[64,16]{0,1:T(8,128)S(1)}, f32[64,16]{0,1:T(8,128)S(1)}, u32[]{:S(2)}, u32[]{:S(2)}) %collective-permute-start.6) | collective-permute-done | bytes 4128 | tf_op jit(solution)/shard_map/ppermute | solution.py:79
  60.0 6.4 %scatter_custom_fusion = f32[128,1152]{1,0:T(8,128)S(1)} fusion(s32[512]{0:T(512)S(1)} %compare_select_fusion, f32[512,1152]{1,0:T(8,128)} %copy.44, f32[]{:T(128)} %constant.59.clone.1), kind=kCustom, calls=%fused_computation.104 | custom fusion | flops 589824 | bytes 590336 | tf_op jit(solution)/shard_map/scatter-add | solution.py:48
  67.5 3.3 %collective-permute-start.8 = (f32[1,72,16,128]{3,1,2,0:T(8,128)S(1)}, f32[1,72,16,128]{3,1,2,0:T(8,128)S(1)}, u32[]{:S(2)}, u32[]{:S(2)}) collective-permute-start(f32[1,72,16,128]{3,1,2,0:T(8,128)S(1)} %convolution_bitcast_fusion.3), channel_id=1, source_target_pairs={{1,0},{2,1},{3,2},{8,3},{9,8},{10,9},{11,10},{16,11},{17,16},{18,1... | collective-permute-start | bytes 1769480 | tf_op jit(solution)/shard_map/ppermute | solution.py:18
  70.8 4.1 %all-to-all-start = ((f32[4,18,2,128]{3,2,1,0:T(2,128)}), f32[4,18,2,128]{3,2,1,0:T(2,128)S(1)}, u32[]{:S(2)}, u32[]{:S(2)}) async-start(f32[4,18,2,128]{3,2,1,0:T(2,128)} %param.7), calls=%async_computation | async-start | bytes 147456 | tf_op jit(solution)/shard_map/all_to_all | solution.py:93
  74.9 22.7 %all-to-all-done = f32[4,18,2,128]{3,2,1,0:T(2,128)S(1)} async-done(((f32[4,18,2,128]{3,2,1,0:T(2,128)}), f32[4,18,2,128]{3,2,1,0:T(2,128)S(1)}, u32[]{:S(2)}, u32[]{:S(2)}) %all-to-all-start) | async-done | bytes 73760 | tf_op jit(solution)/shard_map/all_to_all | solution.py:93
  101.2 2.0 copy.49
  107.7 2.7 %convolution_bitcast_fusion.2 = f32[1,72,16,128]{3,1,2,0:T(8,128)S(1)} fusion(f32[1,72,16,128]{3,1,2,0:T(8,128)S(1)} %convolution_bitcast_fusion.3, f32[1,72,16,128]{3,1,2,0:T(8,128)} %copy-done.1, f32[1,72,16,128]{3,1,2,0:T(8,128)} %copy-done.2, f32[3,72,16,1]{3,1,2,0:T(8,128)} %copy.52, f32[3,72,16,1]{3,1,2,0:T(8,128)S(1)} %copy.50, ...), kind=kOutput, calls=%fused_computation.7 | convolution fusion | flops 130351104 | bytes 2555138 | tf_op jit(solution)/shard_map/rjk,rjtl->rktl/dot_general | solution.py:43
  110.3 4.1 %collective-permute-start.12 = (f32[1,72,16,128]{3,1,2,0:T(8,128)S(1)}, f32[1,72,16,128]{3,1,2,0:T(8,128)S(1)}, u32[]{:S(2)}, u32[]{:S(2)}) collective-permute-start(f32[1,72,16,128]{3,1,2,0:T(8,128)S(1)} %convolution_bitcast_fusion.2), channel_id=1, source_target_pairs={{1,0},{2,1},{3,2},{8,3},{9,8},{10,9},{11,10},{16,11},{17,16},{18,1... | collective-permute-start | bytes 1769480 | tf_op jit(solution)/shard_map/ppermute | solution.py:18
  114.5 13.7 %collective-permute-done.12 = f32[1,72,16,128]{3,1,2,0:T(8,128)S(1)} collective-permute-done((f32[1,72,16,128]{3,1,2,0:T(8,128)S(1)}, f32[1,72,16,128]{3,1,2,0:T(8,128)S(1)}, u32[]{:S(2)}, u32[]{:S(2)}) %collective-permute-start.12) | collective-permute-done | bytes 589856 | tf_op jit(solution)/shard_map/ppermute | solution.py:18
  128.2 13.2 %collective-permute-done.11 = f32[1,72,16,128]{3,1,2,0:T(8,128)S(1)} collective-permute-done((f32[1,72,16,128]{3,1,2,0:T(8,128)S(1)}, f32[1,72,16,128]{3,1,2,0:T(8,128)S(1)}, u32[]{:S(2)}, u32[]{:S(2)}) %collective-permute-start.11) | collective-permute-done | bytes 589856 | tf_op jit(solution)/shard_map/ppermute | solution.py:15
  150.1 2.7 %convolution_bitcast_fusion.1 = f32[1,72,16,128]{3,1,2,0:T(8,128)S(1)} fusion(f32[1,72,16,128]{3,1,2,0:T(8,128)S(1)} %convolution_bitcast_fusion.2, f32[1,72,16,128]{3,1,2,0:T(8,128)} %copy-done.4, f32[1,72,16,128]{3,1,2,0:T(8,128)} %copy-done.6, f32[3,72,16,1]{3,1,2,0:T(8,128)} %copy.58, f32[3,72,16,1]{3,1,2,0:T(8,128)S(1)} %copy.56, ...), kind=kOutput, calls=%fused_computation.6 | convolution fusion | flops 130351104 | bytes 2555138 | tf_op jit(solution)/shard_map/rjk,rjtl->rktl/dot_general | solution.py:43
  154.8 14.0 %collective-permute-done.16 = f32[1,72,16,128]{3,1,2,0:T(8,128)S(1)} collective-permute-done((f32[1,72,16,128]{3,1,2,0:T(8,128)S(1)}, f32[1,72,16,128]{3,1,2,0:T(8,128)S(1)}, u32[]{:S(2)}, u32[]{:S(2)}) %collective-permute-start.16) | collective-permute-done | bytes 589856 | tf_op jit(solution)/shard_map/ppermute | solution.py:18
  168.8 12.4 %collective-permute-done.15 = f32[1,72,16,128]{3,1,2,0:T(8,128)S(1)} collective-permute-done((f32[1,72,16,128]{3,1,2,0:T(8,128)S(1)}, f32[1,72,16,128]{3,1,2,0:T(8,128)S(1)}, u32[]{:S(2)}, u32[]{:S(2)}) %collective-permute-start.15) | collective-permute-done | bytes 589856 | tf_op jit(solution)/shard_map/ppermute | solution.py:15
  189.9 2.7 %convolution_bitcast_fusion = f32[1,72,16,128]{3,1,2,0:T(8,128)S(1)} fusion(f32[1,72,16,128]{3,1,2,0:T(8,128)S(1)} %convolution_bitcast_fusion.1, f32[1,72,16,128]{3,1,2,0:T(8,128)} %copy-done.5, f32[1,72,16,128]{3,1,2,0:T(8,128)} %copy-done.7, f32[3,72,16,1]{3,1,2,0:T(8,128)} %copy.63, f32[3,72,16,1]{3,1,2,0:T(8,128)S(1)} %copy.61, ...), kind=kOutput, calls=%fused_computation.5 | convolution fusion | flops 130351104 | bytes 2555138 | tf_op jit(solution)/shard_map/rjk,rjtl->rktl/dot_general | solution.py:43
  192.6 2.9 %collective-permute-start.20 = (f32[1,72,16,128]{3,1,2,0:T(8,128)S(1)}, f32[1,72,16,128]{3,1,2,0:T(8,128)S(1)}, u32[]{:S(2)}, u32[]{:S(2)}) collective-permute-start(f32[1,72,16,128]{3,1,2,0:T(8,128)S(1)} %convolution_bitcast_fusion), channel_id=1, source_target_pairs={{1,0},{2,1},{3,2},{8,3},{9,8},{10,9},{11,10},{16,11},{17,16},{18,1... | collective-permute-start | bytes 1769480 | tf_op jit(solution)/shard_map/ppermute | solution.py:18
  195.5 13.7 %collective-permute-done.20 = f32[1,72,16,128]{3,1,2,0:T(8,128)S(1)} collective-permute-done((f32[1,72,16,128]{3,1,2,0:T(8,128)S(1)}, f32[1,72,16,128]{3,1,2,0:T(8,128)S(1)}, u32[]{:S(2)}, u32[]{:S(2)}) %collective-permute-start.20) | collective-permute-done | bytes 589856 | tf_op jit(solution)/shard_map/ppermute | solution.py:18
  209.2 14.2 %collective-permute-done.19 = f32[1,72,16,128]{3,1,2,0:T(8,128)S(1)} collective-permute-done((f32[1,72,16,128]{3,1,2,0:T(8,128)S(1)}, f32[1,72,16,128]{3,1,2,0:T(8,128)S(1)}, u32[]{:S(2)}, u32[]{:S(2)}) %collective-permute-start.19) | collective-permute-done | bytes 589856 | tf_op jit(solution)/shard_map/ppermute | solution.py:15
  226.3 2.0 copy.65
  234.1 19.1 %all_to_all.24 = f32[1,72,16,128]{3,2,0,1:T(8,128)S(1)} all-to-all(f32[1,72,16,128]{3,2,0,1:T(8,128)S(1)} %copy.69), channel_id=1, replica_groups=mesh['lat'=4,'lon'=2,'lev'=4] {'lev'}, dimensions={1} | all-to-all | bytes 1179648 | tf_op jit(solution)/shard_map/all_to_all | solution.py:102
  (100 shorter events, 49.7 us)
Async XLA Ops:
  1.4 44.9 %collective-permute-start.1 = (f32[64,16]{0,1:T(8,128)S(1)}, f32[64,16]{0,1:T(8,128)S(1)}, u32[]{:S(2)}, u32[]{:S(2)}) collective-permute-start(f32[64,16]{0,1:T(8,128)S(1)} %broadcast_multiply_fusion.2), channel_id=1, source_target_pairs={{0,7},{1,0},{2,1},{3,2},{4,3},{5,4},{6,5},{7,6},{8,15},{9,8},{10,9... | collective-permute-start | bytes 12296 | tf_op jit(solution)/shard_map/ppermute | solution.py:84
  5.9 12.9 %collective-permute-start = (f32[64,16]{0,1:T(8,128)S(1)}, f32[64,16]{0,1:T(8,128)S(1)}, u32[]{:S(2)}, u32[]{:S(2)}) collective-permute-start(f32[64,16]{0,1:T(8,128)S(1)} %broadcast_multiply_fusion.2), channel_id=1, source_target_pairs={{0,1},{1,2},{2,3},{3,4},{4,5},{5,6},{6,7},{7,0},{8,9},{9,10},{10,1... | collective-permute-start | bytes 12296 | tf_op jit(solution)/shard_map/ppermute | solution.py:79
  18.7 29.1 %collective-permute-start.2 = (f32[64,16]{0,1:T(8,128)S(1)}, f32[64,16]{0,1:T(8,128)S(1)}, u32[]{:S(2)}, u32[]{:S(2)}) collective-permute-start(f32[64,16]{0,1:T(8,128)S(1)} %collective-permute-done), channel_id=1, source_target_pairs={{0,1},{1,2},{2,3},{3,4},{4,5},{5,6},{6,7},{7,0},{8,9},{9,10},{10,1... | collective-permute-start | bytes 12296 | tf_op jit(solution)/shard_map/ppermute | solution.py:79
  46.3 3.7 %collective-permute-start.3 = (f32[64,16]{0,1:T(8,128)S(1)}, f32[64,16]{0,1:T(8,128)S(1)}, u32[]{:S(2)}, u32[]{:S(2)}) collective-permute-start(f32[64,16]{0,1:T(8,128)S(1)} %collective-permute-done.1), channel_id=1, source_target_pairs={{0,7},{1,0},{2,1},{3,2},{4,3},{5,4},{6,5},{7,6},{8,15},{9,8},{10,9... | collective-permute-start | bytes 12296 | tf_op jit(solution)/shard_map/ppermute | solution.py:84
  47.8 4.9 %collective-permute-start.4 = (f32[64,16]{0,1:T(8,128)S(1)}, f32[64,16]{0,1:T(8,128)S(1)}, u32[]{:S(2)}, u32[]{:S(2)}) collective-permute-start(f32[64,16]{0,1:T(8,128)S(1)} %collective-permute-done.2), channel_id=1, source_target_pairs={{0,1},{1,2},{2,3},{3,4},{4,5},{5,6},{6,7},{7,0},{8,9},{9,10},{10,1... | collective-permute-start | bytes 12296 | tf_op jit(solution)/shard_map/ppermute | solution.py:79
  49.9 4.6 %collective-permute-start.5 = (f32[64,16]{0,1:T(8,128)S(1)}, f32[64,16]{0,1:T(8,128)S(1)}, u32[]{:S(2)}, u32[]{:S(2)}) collective-permute-start(f32[64,16]{0,1:T(8,128)S(1)} %collective-permute-done.3), channel_id=1, source_target_pairs={{0,7},{1,0},{2,1},{3,2},{4,3},{5,4},{6,5},{7,6},{8,15},{9,8},{10,9... | collective-permute-start | bytes 12296 | tf_op jit(solution)/shard_map/ppermute | solution.py:84
  52.7 4.9 %collective-permute-start.6 = (f32[64,16]{0,1:T(8,128)S(1)}, f32[64,16]{0,1:T(8,128)S(1)}, u32[]{:S(2)}, u32[]{:S(2)}) collective-permute-start(f32[64,16]{0,1:T(8,128)S(1)} %collective-permute-done.4), channel_id=1, source_target_pairs={{0,1},{1,2},{2,3},{3,4},{4,5},{5,6},{6,7},{7,0},{8,9},{9,10},{10,1... | collective-permute-start | bytes 12296 | tf_op jit(solution)/shard_map/ppermute | solution.py:79
  67.5 30.1 %collective-permute-start.8 = (f32[1,72,16,128]{3,1,2,0:T(8,128)S(1)}, f32[1,72,16,128]{3,1,2,0:T(8,128)S(1)}, u32[]{:S(2)}, u32[]{:S(2)}) collective-permute-start(f32[1,72,16,128]{3,1,2,0:T(8,128)S(1)} %convolution_bitcast_fusion.3), channel_id=1, source_target_pairs={{1,0},{2,1},{3,2},{8,3},{9,8},{10,9},{11,10},{16,11},{17,16},{18,1... | collective-permute-start | bytes 1769480 | tf_op jit(solution)/shard_map/ppermute | solution.py:18
  70.8 26.9 %collective-permute-start.7 = (f32[1,72,16,128]{3,1,2,0:T(8,128)S(1)}, f32[1,72,16,128]{3,1,2,0:T(8,128)S(1)}, u32[]{:S(2)}, u32[]{:S(2)}) collective-permute-start(f32[1,72,16,128]{3,1,2,0:T(8,128)S(1)} %convolution_bitcast_fusion.3), channel_id=1, source_target_pairs={{0,1},{1,2},{2,3},{3,8},{8,9},{9,10},{10,11},{11,16},{16,17},{17,1... | collective-permute-start | bytes 1769480 | tf_op jit(solution)/shard_map/ppermute | solution.py:15
  70.8 26.8 %all-to-all-start = ((f32[4,18,2,128]{3,2,1,0:T(2,128)}), f32[4,18,2,128]{3,2,1,0:T(2,128)S(1)}, u32[]{:S(2)}, u32[]{:S(2)}) async-start(f32[4,18,2,128]{3,2,1,0:T(2,128)} %param.7), calls=%async_computation | async-start | bytes 147456 | tf_op jit(solution)/shard_map/all_to_all | solution.py:93
  103.8 2.0 collective-permute-start.10
  103.9 1.3 collective-permute-start.9
  110.3 17.8 %collective-permute-start.12 = (f32[1,72,16,128]{3,1,2,0:T(8,128)S(1)}, f32[1,72,16,128]{3,1,2,0:T(8,128)S(1)}, u32[]{:S(2)}, u32[]{:S(2)}) collective-permute-start(f32[1,72,16,128]{3,1,2,0:T(8,128)S(1)} %convolution_bitcast_fusion.2), channel_id=1, source_target_pairs={{1,0},{2,1},{3,2},{8,3},{9,8},{10,9},{11,10},{16,11},{17,16},{18,1... | collective-permute-start | bytes 1769480 | tf_op jit(solution)/shard_map/ppermute | solution.py:18
  114.5 26.9 %collective-permute-start.11 = (f32[1,72,16,128]{3,1,2,0:T(8,128)S(1)}, f32[1,72,16,128]{3,1,2,0:T(8,128)S(1)}, u32[]{:S(2)}, u32[]{:S(2)}) collective-permute-start(f32[1,72,16,128]{3,1,2,0:T(8,128)S(1)} %convolution_bitcast_fusion.2), channel_id=1, source_target_pairs={{0,1},{1,2},{2,3},{3,8},{8,9},{9,10},{10,11},{11,16},{16,17},{17,1... | collective-permute-start | bytes 1769480 | tf_op jit(solution)/shard_map/ppermute | solution.py:15
  146.2 1.2 collective-permute-start.13
  146.9 1.4 collective-permute-start.14
  152.8 16.1 %collective-permute-start.16 = (f32[1,72,16,128]{3,1,2,0:T(8,128)S(1)}, f32[1,72,16,128]{3,1,2,0:T(8,128)S(1)}, u32[]{:S(2)}, u32[]{:S(2)}) collective-permute-start(f32[1,72,16,128]{3,1,2,0:T(8,128)S(1)} %convolution_bitcast_fusion.1), channel_id=1, source_target_pairs={{1,0},{2,1},{3,2},{8,3},{9,8},{10,9},{11,10},{16,11},{17,16},{18,1... | collective-permute-start | bytes 1769480 | tf_op jit(solution)/shard_map/ppermute | solution.py:18
  154.6 26.7 %collective-permute-start.15 = (f32[1,72,16,128]{3,1,2,0:T(8,128)S(1)}, f32[1,72,16,128]{3,1,2,0:T(8,128)S(1)}, u32[]{:S(2)}, u32[]{:S(2)}) collective-permute-start(f32[1,72,16,128]{3,1,2,0:T(8,128)S(1)} %convolution_bitcast_fusion.1), channel_id=1, source_target_pairs={{0,1},{1,2},{2,3},{3,8},{8,9},{9,10},{10,11},{11,16},{16,17},{17,1... | collective-permute-start | bytes 1769480 | tf_op jit(solution)/shard_map/ppermute | solution.py:15
  186.1 1.2 collective-permute-start.17
  186.7 1.4 collective-permute-start.18
  192.6 16.6 %collective-permute-start.20 = (f32[1,72,16,128]{3,1,2,0:T(8,128)S(1)}, f32[1,72,16,128]{3,1,2,0:T(8,128)S(1)}, u32[]{:S(2)}, u32[]{:S(2)}) collective-permute-start(f32[1,72,16,128]{3,1,2,0:T(8,128)S(1)} %convolution_bitcast_fusion), channel_id=1, source_target_pairs={{1,0},{2,1},{3,2},{8,3},{9,8},{10,9},{11,10},{16,11},{17,16},{18,1... | collective-permute-start | bytes 1769480 | tf_op jit(solution)/shard_map/ppermute | solution.py:18
  195.5 27.9 %collective-permute-start.19 = (f32[1,72,16,128]{3,1,2,0:T(8,128)S(1)}, f32[1,72,16,128]{3,1,2,0:T(8,128)S(1)}, u32[]{:S(2)}, u32[]{:S(2)}) collective-permute-start(f32[1,72,16,128]{3,1,2,0:T(8,128)S(1)} %convolution_bitcast_fusion), channel_id=1, source_target_pairs={{0,1},{1,2},{2,3},{3,8},{8,9},{9,10},{10,11},{11,16},{16,17},{17,1... | collective-permute-start | bytes 1769480 | tf_op jit(solution)/shard_map/ppermute | solution.py:15
  228.3 1.2 collective-permute-start.21
  228.9 1.4 collective-permute-start.22
  (8 other events, 96.4 us)
